TPU v7x, 512 devices: a whole 4x8x8 slice. The times are simulated.
512 devices in a mesh: row: 16 (over x, z_hi), col: 32 (over z_lo, y, core).
Axes of the slice: x: 4, y: 8, z: 8 (z_hi: 4, z_lo: 2; z = z_hi * 2 + z_lo), core: 2. Of those that a mesh axis runs over, the one named last changes fastest.
Arguments:
- bin_features: bfloat16 [4096, 512], P('row'), may hold values from -6 to 6
- w_left: bfloat16 [512, 32], replicated, may hold values from -0.25 to 0.25
- w_right: bfloat16 [512, 32], replicated, may hold values from -0.25 to 0.25
- depth_kernel: float32 [9, 32], replicated, may hold values from -2 to 2
- w_point: bfloat16 [32, 32], replicated, may hold values from -1 to 1
- w_head: bfloat16 [32, 24], replicated, may hold values from -1 to 1
- cotangent: bfloat16 [24, 4096, 4096], P(None, 'row', 'col'), may hold values from -6 to 6
Outputs:
- grad_features: bfloat16 [4096, 512], P('row')
- grad_w_left: float32 [512, 32], replicated
- grad_w_right: float32 [512, 32], replicated
- grad_kernel: float32 [9, 32], replicated
- grad_point: float32 [32, 32], replicated
- grad_head: float32 [32, 24], replicated
All inputs are finite; a program needn't handle non-finite values.
Results may differ from a plain program's by a relative error of at most 0.019.
Values may be sent and summed in bfloat16 or wider, within the bound.
No kernel may reach another device: no remote copies, remote signals or barrier semaphores. Data moves between devices by JAX's collectives and lax.ppermute only.
A program may use at most 64 MiB of HBM per device.

v0:
```python
import math
import jax
import jax.numpy as jnp
from jax import lax
from jax.sharding import PartitionSpec as P

DILATION_STEP = 4


def from_root(block, axis, source):
    block = jnp.where(lax.axis_index(axis) == source, block, jnp.zeros_like(block))
    return lax.psum(block, axis)


def extended(x, sides, width):
    for axis, dim in sides:
        count, length = (lax.axis_size(axis), x.shape[dim])
        up = [(i, (i + 1) % count) for i in range(count - 1)]
        down = [(j, i) for i, j in up]
        last = lax.slice_in_dim(x, length - width, length, axis=dim)
        first = lax.slice_in_dim(x, 0, width, axis=dim)
        before = lax.ppermute(last, axis, up)
        after = lax.ppermute(first, axis, down)
        x = jnp.concatenate([before, x, after], axis=dim)
    return x


def silu_slope(values):
    logistic = jax.nn.sigmoid(values)
    return logistic * (1.0 + values * (1.0 - logistic))


def depthwise(kernel_taps, padded, output_rows, output_columns):
    result = jnp.zeros((padded.shape[0], output_rows, output_columns), jnp.float32)
    for kernel_tap_row in range(3):
        for kernel_tap_column in range(3):
            result = result + kernel_taps[3 * kernel_tap_row + kernel_tap_column][
                :, None, None
            ] * padded[
                :,
                DILATION_STEP * kernel_tap_row : DILATION_STEP * kernel_tap_row + output_rows,
                DILATION_STEP * kernel_tap_column : DILATION_STEP * kernel_tap_column
                + output_columns,
            ].astype(
                jnp.float32
            )
    return result


def body(bin_features, w_left, w_right, depth_kernel, w_point, w_head, cotangent):
    rows_per_tile = bin_features.shape[0]
    columns_per_tile = cotangent.shape[2]
    chans = w_left.shape[1]
    row_count = lax.axis_size("row")
    col_count = lax.axis_size("col")
    panel_ratio = col_count // row_count
    contact_map_bins = rows_per_tile * row_count
    grad_scale = 1.0 / math.sqrt(contact_map_bins)
    row_index = lax.axis_index("row")
    col_index = lax.axis_index("col")
    left_panel = jnp.dot(bin_features, w_left, preferred_element_type=jnp.float32).astype(
        jnp.bfloat16
    )
    offset = col_index % panel_ratio * columns_per_tile
    own_rows = lax.dynamic_slice_in_dim(bin_features, offset, columns_per_tile, 0)
    right_own = jnp.dot(own_rows, w_right, preferred_element_type=jnp.float32).astype(jnp.bfloat16)
    right_panel = from_root(right_own, "row", col_index // panel_ratio)
    pair_matrix = (
        left_panel.astype(jnp.float32).T[:, :, None] + right_panel.astype(jnp.float32).T[:, None, :]
    ).astype(jnp.bfloat16)
    extended_pair = extended(pair_matrix, (("row", 1), ("col", 2)), DILATION_STEP)
    convolved_map = depthwise(depth_kernel, extended_pair, rows_per_tile, columns_per_tile)
    trunk_gradient = (
        grad_scale
        * jnp.einsum("ch,hij->cij", w_head, cotangent, preferred_element_type=jnp.float32)
    ).astype(jnp.bfloat16)
    grad_hidden = jnp.einsum(
        "co,oij->cij", w_point, trunk_gradient, preferred_element_type=jnp.float32
    )
    convolved_gradient = (grad_hidden * silu_slope(convolved_map)).astype(jnp.bfloat16)
    extended_gradient = extended(convolved_gradient, (("row", 1), ("col", 2)), DILATION_STEP)
    hidden_state = jax.nn.silu(convolved_map).astype(jnp.bfloat16)
    mixed_out = jnp.einsum("co,cij->oij", w_point, hidden_state, preferred_element_type=jnp.float32)
    centre_offset = extended_pair[
        :,
        DILATION_STEP : DILATION_STEP + rows_per_tile,
        DILATION_STEP : DILATION_STEP + columns_per_tile,
    ]
    trunk_matrix = (centre_offset.astype(jnp.float32) + mixed_out).astype(jnp.bfloat16)
    conv_f32 = convolved_gradient.astype(jnp.float32)
    backward_pass = jnp.zeros((chans, rows_per_tile, columns_per_tile), jnp.float32)
    kern_terms = []
    for kernel_tap_row in range(3):
        for kernel_tap_column in range(3):
            backward_pass = backward_pass + depth_kernel[3 * kernel_tap_row + kernel_tap_column][
                :, None, None
            ] * extended_gradient[
                :,
                DILATION_STEP * (2 - kernel_tap_row) : DILATION_STEP * (2 - kernel_tap_row)
                + rows_per_tile,
                DILATION_STEP * (2 - kernel_tap_column) : DILATION_STEP * (2 - kernel_tap_column)
                + columns_per_tile,
            ].astype(
                jnp.float32
            )
            shifted_window = extended_pair[
                :,
                DILATION_STEP * kernel_tap_row : DILATION_STEP * kernel_tap_row + rows_per_tile,
                DILATION_STEP * kernel_tap_column : DILATION_STEP * kernel_tap_column
                + columns_per_tile,
            ].astype(jnp.float32)
            kern_terms.append(jnp.sum(conv_f32 * shifted_window, axis=(1, 2)))
    kernel_part = jnp.stack(kern_terms)
    pair_gradient = trunk_gradient.astype(jnp.float32) + backward_pass
    left_part = jnp.sum(pair_gradient, axis=2).T
    right_part = jnp.sum(pair_gradient, axis=1).T
    point_part = jnp.einsum(
        "fsk,gsk->fg", hidden_state, trunk_gradient, preferred_element_type=jnp.float32
    )
    head_part = jnp.einsum(
        "ydq,gdq->yg", trunk_matrix, cotangent, preferred_element_type=jnp.float32
    )
    grad_left = lax.psum(left_part, "col").astype(jnp.bfloat16)
    column_total = lax.psum(right_part, "row").astype(jnp.bfloat16)
    all_panels = lax.all_gather(column_total, "col", axis=0, tiled=True)
    grad_right = lax.dynamic_slice_in_dim(all_panels, row_index * rows_per_tile, rows_per_tile, 0)
    grad_features = (
        jnp.dot(grad_left, w_left.T, preferred_element_type=jnp.float32)
        + jnp.dot(grad_right, w_right.T, preferred_element_type=jnp.float32)
    ).astype(jnp.bfloat16)
    contract = (((0,), (0,)), ((), ()))
    wleft_part = lax.dot_general(
        bin_features, grad_left, contract, preferred_element_type=jnp.float32
    )
    wright_part = lax.dot_general(
        bin_features, grad_right, contract, preferred_element_type=jnp.float32
    )
    kernel_sum, point_sum, head_sum = lax.psum((kernel_part, point_part, head_part), ("row", "col"))
    wleft_sum, wright_sum = lax.psum((wleft_part, wright_part), "row")
    return (
        grad_features,
        grad_scale * wleft_sum,
        grad_scale * wright_sum,
        grad_scale * kernel_sum,
        grad_scale * point_sum,
        grad_scale * head_sum,
    )


def solution(mesh):
    placed = (P("row", None), P(), P(), P(), P(), P(), P(None, "row", "col"))
    return jax.shard_map(
        body,
        mesh=mesh,
        in_specs=placed,
        out_specs=(P("row", None), P(), P(), P(), P(), P()),
        check_vma=False,
    )
```

profile of v0, /device:TPU:8, one launch (start us, length us, event | category | flops | bytes accessed | tf_op | source)
XLA Modules:
  0.0 674.3 jit_solution(18254187634809960480)
XLA Ops:
  8.4 50.8 %psum.56 = bf16[32,128]{1,0:T(8,128)(2,1)S(1)} all-reduce(bf16[32,128]{1,0:T(8,128)(2,1)S(1)} %fusion.34), channel_id=1, replica_groups=mesh['row'=16,'col'=32] {'row'}, use_global_device_ids=true, to_apply=%region_0.1 | all-reduce | flops 4096 | bytes 16384 | tf_op jit(solution)/shard_map/psum | solution.py:12
  64.8 3.5 multiply_convert_fusion.1
  73.5 3.6 copy.20
  77.1 3.6 copy.22
  85.3 3.3 collective-permute-done.2
  88.6 3.0 copy.21
  91.6 3.0 copy.23
  94.7 7.2 %maximum_maximum_fusion = (bf16[32,264,132]{2,0,1:T(8,128)(2,1)S(1)}, bf16[32,264,132]{2,0,1:T(8,128)(2,1)S(1)}) fusion(bf16[32,4,128]{2,0,1:T(8,128)(2,1)S(1)} %collective-permute-done.1, bf16[32,256,128]{2,0,1:T(8,128)(2,1)} %copy-done.1, bf16[32,4,128]{2,0,1:T(8,128)(2,1)S(1)} %collective-permute-done, bf16[32,264,4]{2,0,1:T(8,128)(2,1)} %copy.21, ...), kind=kLoop, calls=%fused_computation.20 | loop fusion | flops 17842176 | bytes 6758400 | tf_op jit(solution)/shard_map/concatenate | solution.py:24
  101.9 10.2 %multiply_convert_fusion = (bf16[32,256,128]{2,0,1:T(8,128)(2,1)}, f32[32,256,128]{2,0,1:T(8,128)}) fusion(bf16[32,264,132]{2,0,1:T(8,128)(2,1)S(1)} %get-tuple-element.34, f32[32]{0:T(128)S(1)} %get-tuple-element.48, bf16[32,4,128]{2,0,1:T(8,128)(2,1)S(1)} %collective-permute-done.1, bf16[32,256,128]{2,0,1:T(8,128)(2,1)S(1)} %copy-done.2, ...), kind=kLoop, calls=%fused_computation.50 | loop fusion | flops 36700160 | bytes 21087360 | tf_op jit(solution)/shard_map/convert_element_type | solution.py:82
  112.1 3.4 fusion.30
  115.6 3.0 convolution_bitcast_fusion.2
  119.0 13.2 %fusion.23 = (f32[32]{0:T(128)S(1)}, f32[32]{0:T(128)S(1)}, f32[32]{0:T(128)S(1)}, f32[32]{0:T(128)S(1)}, f32[32]{0:T(128)S(1)}, /*index=5*/f32[32]{0:T(128)S(1)...) fusion(bf16[32,264,132]{2,0,1:T(8,128)(2,1)} %copy-done.5, ...), kind=kOutput, calls=%fused_computation.47 | convolution fusion | flops 110100192 | bytes 23186560 | tf_op jit(solution)/shard_map/co,oij->cij/dot_general | solution.py:77
  132.3 96.0 %all-reduce = (f32[9,32]{1,0:T(8,128)S(1)}, f32[32,32]{1,0:T(8,128)S(1)}, f32[32,24]{0,1:T(8,128)S(1)}) all-reduce(f32[9,32]{1,0:T(8,128)S(1)} %stack.39, f32[32,32]{1,0:T(8,128)S(1)} %convolution_bitcast_fusion.2, f32[32,24]{0,1:T(8,128)S(1)} %fusion.30), channel_id=1, replica_groups=mesh['row'=16,'col'=32] {'row','col'}, use_global_device_ids=true, to_apply=%region_16.17 | all-reduce | flops 2080 | bytes 16640 | tf_op jit(solution)/shard_map/psum | solution.py:138
  234.6 5.1 collective-permute-done.5
  244.5 3.6 copy.24
  248.1 3.6 copy.26
  253.7 3.6 collective-permute-start.6
  262.6 3.0 copy.27
  265.6 7.2 %pad_maximum_fusion.1 = (bf16[32,264,132]{2,0,1:T(8,128)(2,1)S(1)}, bf16[32,264,132]{2,0,1:T(8,128)(2,1)S(1)}) fusion(bf16[32,264,4]{2,0,1:T(8,128)(2,1)} %copy.25, bf16[32,4,128]{2,0,1:T(8,128)(2,1)S(1)} %collective-permute-done.5, bf16[32,256,128]{2,0,1:T(8,128)(2,1)} %get-tuple-element.50, bf16[32,4,128]{2,0,1:T(8,128)(2,1)S(1)} %collective-permute-done.4, ...), kind=kLoop, calls=%fused_computation.22 | loop fusion | flops 17842176 | bytes 6758400 | tf_op jit(solution)/shard_map/concatenate | solution.py:24
  272.9 7.2 %fusion.48 = (f32[32,128]{1,0:T(8,128)S(1)}, f32[32,256]{0,1:T(8,128)S(1)}) fusion(bf16[32,264,132]{2,0,1:T(8,128)(2,1)S(1)} %get-tuple-element.30, f32[32]{0:T(128)S(1)} %get-tuple-element.48, bf16[32,256,128]{2,0,1:T(8,128)(2,1)S(1)} %copy-done.6, bf16[32,4,128]{2,0,1:T(8,128)(2,1)S(1)} %collective-permute-done.4, f32[32]{0:T(128)S(1)} %get-tuple-element.49, ...), kind=kLoop, calls=%fused_computation.100 | loop fusion | flops 33542144 | bytes 16893056 | tf_op jit(solution)/shard_map/reduce_sum | solution.py:116
  280.2 102.3 %psum.57 = bf16[256,32]{1,0:T(8,128)(2,1)S(1)} all-reduce(f32[256,32]{1,0:T(8,128)S(1)} %bitcast.73), channel_id=1, replica_groups=mesh['row'=16,'col'=32] {'col'}, use_global_device_ids=true, to_apply=%region_2.3 | all-reduce | flops 8192 | bytes 49152 | tf_op jit(solution)/shard_map/psum | solution.py:123
  383.5 80.7 %psum.58 = bf16[128,32]{0,1:T(8,128)(2,1)S(1)} all-reduce(f32[128,32]{0,1:T(8,128)S(1)} %bitcast.74), channel_id=1, replica_groups=mesh['row'=16,'col'=32] {'row'}, use_global_device_ids=true, to_apply=%region_4.5 | all-reduce | flops 4096 | bytes 24576 | tf_op jit(solution)/shard_map/psum | solution.py:124
  464.2 35.4 %all_gather.3 = bf16[4096,32]{0,1:T(8,128)(2,1)S(1)} all-gather(bf16[128,32]{0,1:T(8,128)(2,1)S(1)} %psum.58), channel_id=1, replica_groups=mesh['row'=16,'col'=32] {'col'}, dimensions={0}, use_global_device_ids=true | all-gather | bytes 270336 | tf_op jit(solution)/shard_map/all_gather | solution.py:125
  501.3 164.6 %all-reduce.4.cloned.1.call-done = (f32[512,32]{0,1:T(8,128)}, f32[512,32]{0,1:T(8,128)}) async-done(((f32[512,32]{0,1:T(8,128)}, f32[512,32]{0,1:T(8,128)}), (f32[512,32]{0,1:T(8,128)}, f32[512,32]{0,1:T(8,128)})) %all-reduce.4.cloned.1.call-update) | async-done | bytes 131088 | tf_op jit(solution)/shard_map/psum | solution.py:139
  (65 shorter events, 39.5 us)
Async XLA Ops:
  7.2 57.7 %copy-start = (bf16[24,256,128]{2,1,0:T(8,128)(2,1)S(1)}, bf16[24,256,128]{2,1,0:T(8,128)(2,1)}, u32[]{:S(2)}) copy-start(bf16[24,256,128]{2,1,0:T(8,128)(2,1)} %param.13) | copy-start | bytes 4718596
  7.2 658.8 %all-reduce.4.cloned.1.call-start = ((), (), s32[]{:S(2)}) async-start(), calls=%async_computation | async-start | bytes 262144 | tf_op jit(solution)/shard_map/psum | solution.py:139
  62.2 8.0 %copy-start.1 = (bf16[32,256,128]{2,0,1:T(8,128)(2,1)}, bf16[32,256,128]{2,0,1:T(8,128)(2,1)S(1)}, u32[]{:S(2)}) copy-start(bf16[32,256,128]{2,0,1:T(8,128)(2,1)S(1)} %add_convert_fusion) | copy-start | bytes 6291460
  62.2 6.1 collective-permute-start
  63.5 6.7 collective-permute-start.1
  73.5 11.8 %copy-start.12 = (f32[9,32]{1,0:T(8,128)S(1)}, f32[9,32]{1,0:T(8,128)}, u32[]{:S(2)}) copy-start(f32[9,32]{1,0:T(8,128)} %param.10) | copy-start | bytes 3460
  80.8 10.9 %collective-permute-start.3 = (bf16[32,264,4]{1,0,2:T(8,128)(2,1)S(1)}, bf16[32,264,4]{1,0,2:T(8,128)(2,1)S(1)}, u32[]{:S(2)}, u32[]{:S(2)}) collective-permute-start(bf16[32,264,4]{1,0,2:T(8,128)(2,1)S(1)} %copy.22), channel_id=1, source_target_pairs={{1,0},{2,1},{3,2},{4,3},{5,4},{6,5},{7,6},{8,7},{9,8},{10,9},{11,1... | collective-permute-start | bytes 202760 | tf_op jit(solution)/shard_map/ppermute | solution.py:23
  82.7 5.9 collective-permute-start.2
  94.7 7.2 %copy-start.2 = (bf16[32,256,128]{2,0,1:T(8,128)(2,1)S(1)}, bf16[32,256,128]{2,0,1:T(8,128)(2,1)}, u32[]{:S(2)}) copy-start(bf16[32,256,128]{2,0,1:T(8,128)(2,1)} %copy-done.1) | copy-start | bytes 6291460
  101.9 10.2 %copy-start.4 = (bf16[32,264,132]{2,0,1:T(8,128)(2,1)}, bf16[32,264,132]{2,0,1:T(8,128)(2,1)S(1)}, u32[]{:S(2)}) copy-start(bf16[32,264,132]{2,0,1:T(8,128)(2,1)S(1)} %get-tuple-element.33) | copy-start | bytes 6690820
  101.9 10.2 %copy-start.5 = (bf16[32,264,132]{2,0,1:T(8,128)(2,1)}, bf16[32,264,132]{2,0,1:T(8,128)(2,1)S(1)}, u32[]{:S(2)}) copy-start(bf16[32,264,132]{2,0,1:T(8,128)(2,1)S(1)} %get-tuple-element.34) | copy-start | bytes 6690820
  101.9 10.2 %copy-start.13 = (bf16[32,32]{1,0:T(8,128)(2,1)S(1)}, bf16[32,32]{1,0:T(8,128)(2,1)}, u32[]{:S(2)}) copy-start(bf16[32,32]{1,0:T(8,128)(2,1)} %param.11) | copy-start | bytes 6148
  115.5 3.1 copy-start.3
  115.5 3.5 copy-start.7
  229.7 4.9 collective-permute-start.4
  232.5 7.2 %collective-permute-start.5 = (bf16[32,4,128]{2,0,1:T(8,128)(2,1)S(1)}, bf16[32,4,128]{2,0,1:T(8,128)(2,1)S(1)}, u32[]{:S(2)}, u32[]{:S(2)}) collective-permute-start(bf16[32,4,128]{2,0,1:T(8,128)(2,1)S(1)} %get-tuple-element.38), channel_id=1, source_target_pairs={{32,0},{64,32},{96,64},{128,96},{160,128},{192,160},{224,192},{256... | collective-permute-start | bytes 98312 | tf_op jit(solution)/shard_map/ppermute | solution.py:23
  251.8 10.8 %collective-permute-start.7 = (bf16[32,264,4]{1,0,2:T(8,128)(2,1)S(1)}, bf16[32,264,4]{1,0,2:T(8,128)(2,1)S(1)}, u32[]{:S(2)}, u32[]{:S(2)}) collective-permute-start(bf16[32,264,4]{1,0,2:T(8,128)(2,1)S(1)} %copy.26), channel_id=1, source_target_pairs={{0,1},{1,2},{2,3},{3,4},{4,5},{5,6},{6,7},{7,8},{8,9},{9,10},{10,1... | collective-permute-start | bytes 202760 | tf_op jit(solution)/shard_map/ppermute | solution.py:22
  253.7 5.8 collective-permute-start.6
  265.6 7.3 %copy-start.6 = (bf16[32,256,128]{2,0,1:T(8,128)(2,1)S(1)}, bf16[32,256,128]{2,0,1:T(8,128)(2,1)}, u32[]{:S(2)}) copy-start(bf16[32,256,128]{2,0,1:T(8,128)(2,1)} %get-tuple-element.50) | copy-start | bytes 6291460
  265.6 7.3 %copy-start.8 = (bf16[32,256,128]{2,0,1:T(8,128)(2,1)S(1)}, bf16[32,256,128]{2,0,1:T(8,128)(2,1)}, u32[]{:S(2)}) copy-start(bf16[32,256,128]{2,0,1:T(8,128)(2,1)} %multiply_convert_fusion.1) | copy-start | bytes 6291460
  272.9 109.6 %copy-start.9 = (bf16[256,512]{1,0:T(8,128)(2,1)S(1)}, bf16[256,512]{1,0:T(8,128)(2,1)}, u32[]{:S(2)}) copy-start(bf16[256,512]{1,0:T(8,128)(2,1)} %param.7) | copy-start | bytes 786436
  272.9 110.4 %copy-start.10 = (bf16[512,32]{0,1:T(8,128)(2,1)S(1)}, bf16[512,32]{0,1:T(8,128)(2,1)}, u32[]{:S(2)}) copy-start(bf16[512,32]{0,1:T(8,128)(2,1)} %param.8) | copy-start | bytes 98308
  272.9 227.5 %copy-start.11 = (bf16[512,32]{0,1:T(8,128)(2,1)S(1)}, bf16[512,32]{0,1:T(8,128)(2,1)}, u32[]{:S(2)}) copy-start(bf16[512,32]{0,1:T(8,128)(2,1)} %param.9) | copy-start | bytes 98308
Sparse Core Ops, SparseCore 0:
  500.5 165.3 all-reduce.3
where the time goes:
time: 675 us; the launch traced here: 674 us
  blocking collectives  365 us (54%)
  waiting for transfers between devices  176 us (26%)
  other arithmetic  39 us (6%)
  local copies, waits for them, and re-layouts  34 us (5%)
  matrix products  28.2 us (4%)
  starting transfers between devices  17 us (3%)
  between operations  14.4 us (2%)
    psum x1, waiting for transfers between devices, body(): wleft_sum, wright_sum = lax.psum((wleft_part, wright_part), 'row')  165 us
    psum x1, blocking collectives, body(): grad_left = lax.psum(left_part, 'col').astype(jnp.bfloat16)  102 us
    psum x1, blocking collectives, body(): lax.psum((kernel_part, point_part, head_part), ('row', 'col'))  96 us
    psum x1, blocking collectives, body(): column_total = lax.psum(right_part, 'row').astype(jnp.bfloat16)  80.7 us
    psum x1, blocking collectives, from_root(): return lax.psum(block, axis)  50.8 us
    all_gather x1, blocking collectives, body(): all_panels = lax.all_gather(column_total, 'col', axis=0, tiled=True)  35.4 us
    concatenate x4, other arithmetic, extended(): x = jnp.concatenate([before, x, after], axis=dim)  16.6 us
  transfers between devices with their start and end apart: 9, of which 5 were waited for; matrix products, arithmetic and copies ran while one was open for 2% of the time, Pallas kernels for 0%

commit v1 on v0

--- a/solution.py
+++ b/solution.py
@@ -121,7 +121,7 @@
         "ydq,gdq->yg", trunk_matrix, cotangent, preferred_element_type=jnp.float32
     )
     grad_left = lax.psum(left_part, "col").astype(jnp.bfloat16)
-    column_total = lax.psum(right_part, "row").astype(jnp.bfloat16)
+    column_total = jnp.sum(lax.all_gather(right_part, "row"), axis=0).astype(jnp.bfloat16)
     all_panels = lax.all_gather(column_total, "col", axis=0, tiled=True)
     grad_right = lax.dynamic_slice_in_dim(all_panels, row_index * rows_per_tile, rows_per_tile, 0)
     grad_features = (

time: 675 us -> 639 us (0.947)
  blocking collectives: 365 us -> 329 us
    psum x1 -> x0, blocking collectives: 80.7 us -> none  [body(): column_total = lax.psum(right_part, 'row').astype(jnp.bfloat16)]
    all_gather x0 -> x1, blocking collectives: none -> 43.8 us  [body(): lax.all_gather(right_part, 'row')]
where the time goes in v1:
time: 639 us; the launch traced here: 638 us
  blocking collectives  329 us (51%)
  waiting for transfers between devices  177 us (28%)
  other arithmetic  39.1 us (6%)
  local copies, waits for them, and re-layouts  34 us (5%)
  matrix products  28.2 us (4%)
  starting transfers between devices  17 us (3%)
  between operations  14.4 us (2%)
    psum x1, waiting for transfers between devices, body(): wleft_sum, wright_sum = lax.psum((wleft_part, wright_part), 'row')  165 us
    psum x1, blocking collectives, body(): grad_left = lax.psum(left_part, 'col').astype(jnp.bfloat16)  102 us
    psum x1, blocking collectives, body(): lax.psum((kernel_part, point_part, head_part), ('row', 'col'))  96 us
    psum x1, blocking collectives, from_root(): return lax.psum(block, axis)  50.8 us
    all_gather x1, blocking collectives, body(): lax.all_gather(right_part, 'row')  43.8 us
    all_gather x1, blocking collectives, body(): all_panels = lax.all_gather(column_total, 'col', axis=0, tiled=True)  35.7 us
    concatenate x4, other arithmetic, extended(): x = jnp.concatenate([before, x, after], axis=dim)  16.6 us
    dot_general x1, matrix products, body(): jnp.einsum('co,oij->cij', w_point, trunk_gradient, preferred_element_type...  13.2 us
  transfers between devices with their start and end apart: 9, of which 5 were waited for; matrix products, arithmetic and copies ran while one was open for 2% of the time, Pallas kernels for 0%

profile of v1, /device:TPU:8, one launch (start us, length us, event | category | flops | bytes accessed | tf_op | source)
XLA Modules:
  0.0 638.0 jit_solution(6885849069666101656)
XLA Ops:
  8.4 50.8 %psum.49 = bf16[32,128]{1,0:T(8,128)(2,1)S(1)} all-reduce(bf16[32,128]{1,0:T(8,128)(2,1)S(1)} %fusion.34), channel_id=1, replica_groups=mesh['row'=16,'col'=32] {'row'}, use_global_device_ids=true, to_apply=%region_0.1 | all-reduce | flops 4096 | bytes 16384 | tf_op jit(solution)/shard_map/psum | solution.py:12
  64.8 3.5 multiply_convert_fusion.1
  73.5 3.6 copy.33
  77.1 3.6 copy.35
  85.3 3.3 collective-permute-done.2
  88.6 3.0 copy.34
  91.6 3.0 copy.36
  94.7 7.2 %maximum_maximum_fusion = (bf16[32,264,132]{2,0,1:T(8,128)(2,1)S(1)}, bf16[32,264,132]{2,0,1:T(8,128)(2,1)S(1)}) fusion(bf16[32,4,128]{2,0,1:T(8,128)(2,1)S(1)} %collective-permute-done.1, bf16[32,256,128]{2,0,1:T(8,128)(2,1)} %copy-done.1, bf16[32,4,128]{2,0,1:T(8,128)(2,1)S(1)} %collective-permute-done, bf16[32,264,4]{2,0,1:T(8,128)(2,1)} %copy.34, ...), kind=kLoop, calls=%fused_computation.20 | loop fusion | flops 17842176 | bytes 6758400 | tf_op jit(solution)/shard_map/concatenate | solution.py:24
  101.9 10.2 %multiply_convert_fusion = (bf16[32,256,128]{2,0,1:T(8,128)(2,1)}, f32[32,256,128]{2,0,1:T(8,128)}) fusion(bf16[32,264,132]{2,0,1:T(8,128)(2,1)S(1)} %get-tuple-element.34, f32[32]{0:T(128)S(1)} %get-tuple-element.48, bf16[32,4,128]{2,0,1:T(8,128)(2,1)S(1)} %collective-permute-done.1, bf16[32,256,128]{2,0,1:T(8,128)(2,1)S(1)} %copy-done.2, ...), kind=kLoop, calls=%fused_computation.50 | loop fusion | flops 36700160 | bytes 21087360 | tf_op jit(solution)/shard_map/convert_element_type | solution.py:82
  112.1 3.4 fusion.30
  115.6 3.0 convolution_bitcast_fusion.2
  119.0 13.2 %fusion.23 = (f32[32]{0:T(128)S(1)}, f32[32]{0:T(128)S(1)}, f32[32]{0:T(128)S(1)}, f32[32]{0:T(128)S(1)}, f32[32]{0:T(128)S(1)}, /*index=5*/f32[32]{0:T(128)S(1)...) fusion(bf16[32,264,132]{2,0,1:T(8,128)(2,1)} %copy-done.5, ...), kind=kOutput, calls=%fused_computation.47 | convolution fusion | flops 110100192 | bytes 23186560 | tf_op jit(solution)/shard_map/co,oij->cij/dot_general | solution.py:77
  132.3 96.0 %all-reduce = (f32[9,32]{1,0:T(8,128)S(1)}, f32[32,32]{1,0:T(8,128)S(1)}, f32[32,24]{0,1:T(8,128)S(1)}) all-reduce(f32[9,32]{1,0:T(8,128)S(1)} %stack.39, f32[32,32]{1,0:T(8,128)S(1)} %convolution_bitcast_fusion.2, f32[32,24]{0,1:T(8,128)S(1)} %fusion.30), channel_id=1, replica_groups=mesh['row'=16,'col'=32] {'row','col'}, use_global_device_ids=true, to_apply=%region_16.17 | all-reduce | flops 2080 | bytes 16640 | tf_op jit(solution)/shard_map/psum | solution.py:138
  234.6 5.1 collective-permute-done.5
  244.5 3.6 copy.37
  248.1 3.6 copy.39
  253.7 3.6 collective-permute-start.6
  262.6 3.0 copy.40
  265.6 7.2 %pad_maximum_fusion.1 = (bf16[32,264,132]{2,0,1:T(8,128)(2,1)S(1)}, bf16[32,264,132]{2,0,1:T(8,128)(2,1)S(1)}) fusion(bf16[32,264,4]{2,0,1:T(8,128)(2,1)} %copy.38, bf16[32,4,128]{2,0,1:T(8,128)(2,1)S(1)} %collective-permute-done.5, bf16[32,256,128]{2,0,1:T(8,128)(2,1)} %get-tuple-element.50, bf16[32,4,128]{2,0,1:T(8,128)(2,1)S(1)} %collective-permute-done.4, ...), kind=kLoop, calls=%fused_computation.22 | loop fusion | flops 17842176 | bytes 6758400 | tf_op jit(solution)/shard_map/concatenate | solution.py:24
  272.9 7.2 %fusion.48 = (f32[32,128]{1,0:T(8,128)S(1)}, f32[32,256]{0,1:T(8,128)S(1)}) fusion(bf16[32,264,132]{2,0,1:T(8,128)(2,1)S(1)} %get-tuple-element.30, f32[32]{0:T(128)S(1)} %get-tuple-element.48, bf16[32,256,128]{2,0,1:T(8,128)(2,1)S(1)} %copy-done.6, bf16[32,4,128]{2,0,1:T(8,128)(2,1)S(1)} %collective-permute-done.4, f32[32]{0:T(128)S(1)} %get-tuple-element.49, ...), kind=kLoop, calls=%fused_computation.101 | loop fusion | flops 33542144 | bytes 16893056 | tf_op jit(solution)/shard_map/reduce_sum | solution.py:116
  280.2 102.3 %psum.50 = bf16[256,32]{1,0:T(8,128)(2,1)S(1)} all-reduce(f32[256,32]{1,0:T(8,128)S(1)} %bitcast.80), channel_id=1, replica_groups=mesh['row'=16,'col'=32] {'col'}, use_global_device_ids=true, to_apply=%region_2.3 | all-reduce | flops 8192 | bytes 49152 | tf_op jit(solution)/shard_map/psum | solution.py:123
  383.5 43.8 %all-gather = f32[2048,32]{0,1:T(8,128)S(1)} all-gather(f32[128,32]{0,1:T(8,128)S(1)} %bitcast.81), channel_id=2, replica_groups=mesh['row'=16,'col'=32] {'row'}, dimensions={0}, use_global_device_ids=true | all-gather | bytes 278528 | tf_op jit(solution)/shard_map/all_gather | solution.py:124
  427.4 35.7 %all_gather.11 = bf16[4096,32]{0,1:T(8,128)(2,1)S(1)} all-gather(bf16[128,32]{0,1:T(8,128)(2,1)S(1)} %bitcast_reduce_fusion), channel_id=1, replica_groups=mesh['row'=16,'col'=32] {'col'}, dimensions={0}, use_global_device_ids=true | all-gather | bytes 270336 | tf_op jit(solution)/shard_map/all_gather | solution.py:125
  464.8 164.8 %all-reduce.4.cloned.1.call-done = (f32[512,32]{0,1:T(8,128)}, f32[512,32]{0,1:T(8,128)}) async-done(((f32[512,32]{0,1:T(8,128)}, f32[512,32]{0,1:T(8,128)}), (f32[512,32]{0,1:T(8,128)}, f32[512,32]{0,1:T(8,128)})) %all-reduce.4.cloned.1.call-update) | async-done | bytes 131088 | tf_op jit(solution)/shard_map/psum | solution.py:139
  (67 shorter events, 39.6 us)
Async XLA Ops:
  7.2 57.7 %copy-start = (bf16[24,256,128]{2,1,0:T(8,128)(2,1)S(1)}, bf16[24,256,128]{2,1,0:T(8,128)(2,1)}, u32[]{:S(2)}) copy-start(bf16[24,256,128]{2,1,0:T(8,128)(2,1)} %param.13) | copy-start | bytes 4718596
  7.2 622.5 %all-reduce.4.cloned.1.call-start = ((), (), s32[]{:S(2)}) async-start(), calls=%async_computation | async-start | bytes 262144 | tf_op jit(solution)/shard_map/psum | solution.py:139
  62.2 8.0 %copy-start.1 = (bf16[32,256,128]{2,0,1:T(8,128)(2,1)}, bf16[32,256,128]{2,0,1:T(8,128)(2,1)S(1)}, u32[]{:S(2)}) copy-start(bf16[32,256,128]{2,0,1:T(8,128)(2,1)S(1)} %add_convert_fusion) | copy-start | bytes 6291460
  62.2 6.1 collective-permute-start
  63.5 6.7 %collective-permute-start.1 = (bf16[32,4,128]{2,0,1:T(8,128)(2,1)S(1)}, bf16[32,4,128]{2,0,1:T(8,128)(2,1)S(1)}, u32[]{:S(2)}, u32[]{:S(2)}) collective-permute-start(bf16[32,4,128]{2,0,1:T(8,128)(2,1)S(1)} %get-tuple-element.40), channel_id=1, source_target_pairs={{32,0},{64,32},{96,64},{128,96},{160,128},{192,160},{224,192},{256... | collective-permute-start | bytes 98312 | tf_op jit(solution)/shard_map/ppermute | solution.py:23
  73.5 11.8 %copy-start.12 = (f32[9,32]{1,0:T(8,128)S(1)}, f32[9,32]{1,0:T(8,128)}, u32[]{:S(2)}) copy-start(f32[9,32]{1,0:T(8,128)} %param.10) | copy-start | bytes 3460
  80.8 10.9 %collective-permute-start.3 = (bf16[32,264,4]{1,0,2:T(8,128)(2,1)S(1)}, bf16[32,264,4]{1,0,2:T(8,128)(2,1)S(1)}, u32[]{:S(2)}, u32[]{:S(2)}) collective-permute-start(bf16[32,264,4]{1,0,2:T(8,128)(2,1)S(1)} %copy.35), channel_id=1, source_target_pairs={{1,0},{2,1},{3,2},{4,3},{5,4},{6,5},{7,6},{8,7},{9,8},{10,9},{11,1... | collective-permute-start | bytes 202760 | tf_op jit(solution)/shard_map/ppermute | solution.py:23
  82.7 5.9 collective-permute-start.2
  94.7 7.2 %copy-start.2 = (bf16[32,256,128]{2,0,1:T(8,128)(2,1)S(1)}, bf16[32,256,128]{2,0,1:T(8,128)(2,1)}, u32[]{:S(2)}) copy-start(bf16[32,256,128]{2,0,1:T(8,128)(2,1)} %copy-done.1) | copy-start | bytes 6291460
  101.9 10.2 %copy-start.4 = (bf16[32,264,132]{2,0,1:T(8,128)(2,1)}, bf16[32,264,132]{2,0,1:T(8,128)(2,1)S(1)}, u32[]{:S(2)}) copy-start(bf16[32,264,132]{2,0,1:T(8,128)(2,1)S(1)} %get-tuple-element.33) | copy-start | bytes 6690820
  101.9 10.2 %copy-start.5 = (bf16[32,264,132]{2,0,1:T(8,128)(2,1)}, bf16[32,264,132]{2,0,1:T(8,128)(2,1)S(1)}, u32[]{:S(2)}) copy-start(bf16[32,264,132]{2,0,1:T(8,128)(2,1)S(1)} %get-tuple-element.34) | copy-start | bytes 6690820
  101.9 10.2 %copy-start.13 = (bf16[32,32]{1,0:T(8,128)(2,1)S(1)}, bf16[32,32]{1,0:T(8,128)(2,1)}, u32[]{:S(2)}) copy-start(bf16[32,32]{1,0:T(8,128)(2,1)} %param.11) | copy-start | bytes 6148
  115.5 3.1 copy-start.3
  115.5 3.5 copy-start.7
  229.7 4.9 collective-permute-start.4
  232.5 7.2 %collective-permute-start.5 = (bf16[32,4,128]{2,0,1:T(8,128)(2,1)S(1)}, bf16[32,4,128]{2,0,1:T(8,128)(2,1)S(1)}, u32[]{:S(2)}, u32[]{:S(2)}) collective-permute-start(bf16[32,4,128]{2,0,1:T(8,128)(2,1)S(1)} %get-tuple-element.38), channel_id=1, source_target_pairs={{32,0},{64,32},{96,64},{128,96},{160,128},{192,160},{224,192},{256... | collective-permute-start | bytes 98312 | tf_op jit(solution)/shard_map/ppermute | solution.py:23
  251.8 10.8 %collective-permute-start.7 = (bf16[32,264,4]{1,0,2:T(8,128)(2,1)S(1)}, bf16[32,264,4]{1,0,2:T(8,128)(2,1)S(1)}, u32[]{:S(2)}, u32[]{:S(2)}) collective-permute-start(bf16[32,264,4]{1,0,2:T(8,128)(2,1)S(1)} %copy.39), channel_id=1, source_target_pairs={{0,1},{1,2},{2,3},{3,4},{4,5},{5,6},{6,7},{7,8},{8,9},{9,10},{10,1... | collective-permute-start | bytes 202760 | tf_op jit(solution)/shard_map/ppermute | solution.py:22
  253.7 5.8 collective-permute-start.6
  265.6 7.3 %copy-start.6 = (bf16[32,256,128]{2,0,1:T(8,128)(2,1)S(1)}, bf16[32,256,128]{2,0,1:T(8,128)(2,1)}, u32[]{:S(2)}) copy-start(bf16[32,256,128]{2,0,1:T(8,128)(2,1)} %get-tuple-element.50) | copy-start | bytes 6291460
  265.6 7.3 %copy-start.8 = (bf16[32,256,128]{2,0,1:T(8,128)(2,1)S(1)}, bf16[32,256,128]{2,0,1:T(8,128)(2,1)}, u32[]{:S(2)}) copy-start(bf16[32,256,128]{2,0,1:T(8,128)(2,1)} %multiply_convert_fusion.1) | copy-start | bytes 6291460
  272.9 109.6 %copy-start.9 = (bf16[256,512]{1,0:T(8,128)(2,1)S(1)}, bf16[256,512]{1,0:T(8,128)(2,1)}, u32[]{:S(2)}) copy-start(bf16[256,512]{1,0:T(8,128)(2,1)} %param.7) | copy-start | bytes 786436
  272.9 110.4 %copy-start.10 = (bf16[512,32]{0,1:T(8,128)(2,1)S(1)}, bf16[512,32]{0,1:T(8,128)(2,1)}, u32[]{:S(2)}) copy-start(bf16[512,32]{0,1:T(8,128)(2,1)} %param.8) | copy-start | bytes 98308
  272.9 190.9 %copy-start.11 = (bf16[512,32]{0,1:T(8,128)(2,1)S(1)}, bf16[512,32]{0,1:T(8,128)(2,1)}, u32[]{:S(2)}) copy-start(bf16[512,32]{0,1:T(8,128)(2,1)} %param.9) | copy-start | bytes 98308
Sparse Core Ops, SparseCore 0:
  464.0 165.6 all-reduce.3
